TPU v7x, 32 devices: a whole 2x2x4 slice. The times are simulated.
32 devices in a mesh: pos: 8 (over z, core), mode: 4 (over y, x).
Axes of the slice: x: 2, y: 2, z: 4, core: 2. Of those that a mesh axis runs over, the one named last changes fastest.
Arguments:
- grid_input: bfloat16 [8, 128, 32, 256], P('mode', 'pos'), may hold values from -6 to 6
- preact: bfloat16 [8, 128, 32, 256], P('mode', 'pos'), may hold values from -6 to 6
- out_grad: bfloat16 [8, 128, 32, 256], P('mode', 'pos'), may hold values from -6 to 6
- mode_weight: bfloat16 [2, 64, 32, 256, 256], P(None, 'mode', 'pos'), may hold values from -0.375 to 0.375
- local_weight: bfloat16 [256, 256], replicated, may hold values from -0.375 to 0.375
Outputs:
- grad_input: bfloat16 [8, 128, 32, 256], P('mode', 'pos')
- grad_modes: bfloat16 [2, 64, 32, 256, 256], P(None, 'mode', 'pos')
All inputs are finite; a program needn't handle non-finite values.
Results may differ from a plain program's by a relative error of at most 0.0087.
Values may be sent and summed in bfloat16 or wider, within the bound.
A program may use at most 128 MiB of HBM per device.

v0:
```python
import functools
import math

import jax
import jax.numpy as jnp
import ml_dtypes
import numpy as np
from jax import lax
from jax.experimental import pallas as pl
from jax.experimental.pallas import tpu as pltpu
from jax.sharding import PartitionSpec as P

MESH = pl.DeviceIdType.MESH
F32 = jnp.float32
BF16 = jnp.bfloat16
GROUP = 128


def twiddle(length, mode_count):
    angles = (np.arange(length)[:, None] * np.arange(mode_count)[None, :] % length) * (2.0 * math.pi / length)
    as_bf16 = lambda v: v.astype(np.float32).astype(ml_dtypes.bfloat16).astype(np.float32)
    return as_bf16(np.cos(angles)), as_bf16(np.sin(angles))


def tables(np_, nm, nb, na, nt, nk, nq):
    cos_t, sin_t = twiddle(nt, np_ * nk)
    cos_s, sin_s = twiddle(np_ * na, nm * nq)
    eye_a, eye_b, eye_m, eye_q = np.eye(na), np.eye(nb), np.eye(nm), np.eye(nq)
    out = lambda v, *shape: jnp.asarray(v.reshape(shape).astype(ml_dtypes.bfloat16))
    by_k = np.stack([cos_t, -sin_t])
    by_k = by_k.reshape(2, nt, np_, nk)
    time_fwd = np.einsum("rtpk,ab->kprabt", by_k, eye_a)
    time_inv = np.einsum("rtpk,ab->katprb", by_k, eye_a)
    fwd = np.stack([np.stack([cos_s, sin_s]), np.stack([-sin_s, cos_s])])
    fwd = fwd.reshape(2, 2, np_, na, nm, nq)
    space_fwd = np.einsum("rspamq,bc->mbrqpcsa", fwd, eye_b)
    inv = np.stack([np.stack([cos_s, -sin_s]), np.stack([sin_s, cos_s])]).reshape(2, 2, np_, na, nm, nq)
    space_inv = np.einsum("rspamq,bc->pbramcsq", inv, eye_b)
    pick = np.einsum("rs,qu,mn,bc->qrmbncsu", np.eye(2), eye_q, eye_m, eye_b)
    turn = np.einsum("rs,qu,mn,bc->qrmbncsu", np.array([[0.0, 1.0], [-1.0, 0.0]]), eye_q, eye_m, eye_b)
    rows = nm * nb * 2 * nq
    pick = pick.reshape(rows, rows)
    return (
        out(time_fwd, nk, np_ * 2 * na, na * nt),
        out(space_fwd, rows, np_ * nb * 2 * na),
        out(pick, rows, rows),
        out(turn, rows, rows),
        out(pick.T, rows, rows),
        out(space_inv, np_ * nb * 2 * na, rows),
        out(time_inv, nk, na * nt, np_ * 2 * na),
    )


def dot(a, b):
    return jnp.dot(a, b, preferred_element_type=F32)


def dot_t(a, b):
    return lax.dot_general(a, b, (((1,), (1,)), ((), ())), preferred_element_type=F32)


def chain_kernel(
    np_, nm, factor,
    pre_hbm, og_hbm, tf_hbm, x_hbm, sf_hbm, pick_hbm, turn_hbm, unpick_hbm, si_hbm, ti_hbm, lw_hbm, w_hbm,
    gi_hbm, xo_hbm, g1_hbm, g2_hbm,
    pre_ref, og_ref, tf_ref, x_ref, sf_ref, pick_ref, turn_ref, unpick_ref, si_ref, ti_ref, lw_ref, w_buf,
    gi_ref, xo_ref, g1_ref, g2_ref,
    slope, acc, gs, gr, xs, xr, ms, mr, ns, nr, bk, bs, br, ts, tr,
    in_sem, out_sem, g_ss, g_rs, x_ss, x_rs, m_ss, m_rs, n_ss, n_rs, b_ss, b_rs, t_ss, t_rs,
):
    nb, rows, c = slope.shape
    _, nk, _, ra, _ = gs.shape
    nq = w_buf.shape[1]
    unit = bk.shape[1] // nq
    pos, mode = lax.axis_index("pos"), lax.axis_index("mode")
    at = {"pos": pos, "mode": mode}
    size = {"pos": np_, "mode": nm}
    peer_of = lambda axis, d: lax.rem(at[axis] + d, size[axis])

    barrier = pltpu.get_barrier_semaphore()
    for axis in ("pos", "mode"):
        for d in range(1, size[axis]):
            pl.semaphore_signal(barrier, inc=1, device_id={axis: peer_of(axis, d)}, device_id_type=MESH)

    hbm = (pre_hbm, og_hbm, tf_hbm, x_hbm, sf_hbm, pick_hbm, turn_hbm, unpick_hbm, si_hbm, ti_hbm, lw_hbm, w_hbm)
    local = (pre_ref, og_ref, tf_ref, x_ref, sf_ref, pick_ref, turn_ref, unpick_ref, si_ref, ti_ref, lw_ref, w_buf)
    loads = [pltpu.make_async_copy(h, v, in_sem.at[n]) for n, (h, v) in enumerate(zip(hbm, local))]
    for load in loads:
        load.start()
    load_of = {id(v): load for v, load in zip(local, loads)}
    ready = lambda *refs: [load_of[id(r)].wait() for r in refs]

    step = 64
    ready(pre_ref, og_ref)

    @pl.loop(0, nb * (rows // step))
    def _(i):
        b, r = i // (rows // step), pl.multiple_of(i % (rows // step) * step, step)
        values = pre_ref[b, pl.ds(r, step), :].astype(F32)
        cdf = 0.5 * (1.0 + lax.erf(values * 0.7071067811865476))
        density = jnp.exp(-0.5 * values * values) * 0.3989422804014327
        grad = og_ref[b, pl.ds(r, step), :].astype(F32)
        slope[b, pl.ds(r, step), :] = (grad * (cdf + values * density)).astype(BF16)

    def copy(axis, peer, slot, k, src, dst, ss, rs):
        return pltpu.make_async_remote_copy(
            src_ref=src.at[peer, k], dst_ref=dst.at[slot, k], send_sem=ss.at[peer, k], recv_sem=rs.at[slot, k],
            device_id={axis: peer}, device_id_type=MESH,
        )

    def send(axis, k, src, dst, ss, rs):
        @pl.loop(1, size[axis])
        def _(d):
            copy(axis, peer_of(axis, d), at[axis], k, src, dst, ss, rs).start()

        dst[at[axis], k] = src[at[axis], k]

    def arrive(axis, k, src, dst, ss, rs):
        @pl.loop(1, size[axis])
        def _(d):
            peer = peer_of(axis, d)
            copy(axis, peer, peer, k, src, dst, ss, rs).wait_recv()

    def drain(axis, k, src, dst, ss, rs):
        @pl.loop(1, size[axis])
        def _(d):
            peer = peer_of(axis, d)
            copy(axis, peer, peer, k, src, dst, ss, rs).wait_send()

    g_way = ("pos", gs, gr, g_ss, g_rs)
    x_way = ("pos", xs, xr, x_ss, x_rs)
    m_way = ("mode", ms, mr, m_ss, m_rs)
    n_way = ("mode", ns, nr, n_ss, n_rs)
    b_way = ("mode", bs, br, b_ss, b_rs)
    t_way = ("pos", ts, tr, t_ss, t_rs)
    go = lambda act, k, way: act(way[0], k, *way[1:])

    def time_fwd(source, buf, k):
        for b in range(nb):
            buf[:, k, b] = dot(tf_ref[k], source[b]).astype(BF16).reshape(np_, ra, c)

    def space_fwd(source, buf, k, scale):
        res = dot(sf_ref[...], source[:, k].reshape(-1, c))
        if scale != 1.0:
            res = res * scale
        buf[:, k] = res.astype(BF16).reshape(nm, -1, c)

    def gathered(buf, k):
        return buf[:, k].reshape(-1, c)

    ready(tf_ref)
    for k in range(nk):
        time_fwd(slope, gs, k)
        if k == 0:
            pl.semaphore_wait(barrier, np_ - 1 + nm - 1)
        go(send, k, g_way)
    ready(x_ref)
    for k in range(nk):
        time_fwd(x_ref, xs, k)
    ready(sf_ref, pick_ref, turn_ref, unpick_ref, si_ref, ti_ref, lw_ref, w_buf)

    stores = []

    def store(n, ref, out):
        stores.append(pltpu.make_async_copy(ref, out, out_sem.at[n]))
        stores[-1].start()

    def stage_space(k):
        go(arrive, k, g_way)
        go(drain, k, g_way)
        go(send, k, x_way)
        space_fwd(gr, ms, k, factor)
        go(send, k, m_way)

    def stage_back(k):
        go(arrive, k, m_way)
        field = gathered(mr, k)
        g1_ref[k] = dot(pick_ref[...], field).astype(BF16)
        g2_ref[k] = dot(turn_ref[...], field).astype(BF16)

        @pl.loop(0, nq, unroll=math.gcd(nq, 4))
        def _(q):
            span = pl.ds(pl.multiple_of(q * unit, unit), unit)
            back = dot_t(g1_ref[k, span, :], w_buf[0, q, k]) + dot_t(g2_ref[k, span, :], w_buf[1, q, k])
            bk[k, span, :] = back.astype(BF16)

        bs[:, k] = dot(unpick_ref[...], bk[k]).astype(BF16).reshape(nm, -1, c)
        go(send, k, b_way)

    def stage_spread(k):
        go(arrive, k, b_way)
        spread = dot(si_ref[...], gathered(br, k)).astype(BF16)
        ts[:, k] = spread.reshape(np_, nb, ra, c)
        go(send, k, t_way)

    def stage_x(k):
        go(arrive, k, x_way)
        space_fwd(xr, ns, k, 1.0)
        go(send, k, n_way)

    def stage_own(k):
        go(arrive, k, n_way)
        xo_ref[k] = dot(pick_ref[...], gathered(nr, k)).astype(BF16)

    def staged(*stages):
        for n in range(nk + len(stages) - 1):
            for lag, stage in enumerate(stages):
                if 0 <= n - lag < nk:
                    stage(n - lag)

    staged(stage_space, stage_back, stage_spread)
    store(0, g1_ref, g1_hbm)
    store(1, g2_ref, g2_hbm)
    for b in range(nb):
        acc[b] = dot_t(slope[b], lw_ref[...])
    staged(stage_x, stage_own)
    store(2, xo_ref, xo_hbm)
    for k in range(nk):
        for way in (x_way, m_way, n_way, b_way):
            go(drain, k, way)

    for k in range(nk):
        go(arrive, k, t_way)
        for b in range(nb):
            part = acc[b] + dot(ti_ref[k], tr[:, k, b].reshape(-1, c))
            if k < nk - 1:
                acc[b] = part
            else:
                gi_ref[b] = part.astype(BF16)
    store(3, gi_ref, gi_hbm)
    for k in range(nk):
        go(drain, k, t_way)
    for copied in stores:
        copied.wait()


def modes_kernel(group, x_hbm, g1_hbm, g2_hbm, gi_hbm, out_hbm, end_hbm, x_ref, g1_ref, g2_ref, gi_ref, buf, in_sem, gi_sem, sem):
    nk, nq, unit, c = x_ref.shape
    pairs = ((x_hbm, x_ref), (g1_hbm, g1_ref), (g2_hbm, g2_ref))
    load = lambda n, k: pltpu.make_async_copy(pairs[n][0].at[k], pairs[n][1].at[k], in_sem.at[n, k])
    for k in range(nk):
        for n in range(3):
            load(n, k).start()
    gi_in = pltpu.make_async_copy(gi_hbm, gi_ref, gi_sem.at[0])
    gi_out = pltpu.make_async_copy(gi_ref, end_hbm, gi_sem.at[1])
    gi_in.start()

    @pl.loop(0, nk)
    def _(k):
        for n in range(3):
            load(n, k).wait()

        @pl.when(k == nk - 1)
        def _():
            gi_in.wait()
            gi_out.start()

        @pl.loop(0, nq // group)
        def _(i):
            first = i * group
            turned = x_ref[k, pl.ds(first, group)].reshape(group * unit, c).T
            for q in range(group):
                for part, g_ref in enumerate((g1_ref, g2_ref)):
                    rows = [jnp.zeros((n * unit, c), BF16) if n else None for n in (q, group - 1 - q)]
                    rows = [v for v in (rows[0], g_ref[k, first + q], rows[1]) if v is not None]
                    field = jnp.concatenate(rows, axis=0) if len(rows) > 1 else rows[0]
                    buf[part, first + q, k] = dot(turned, field).astype(BF16)
                    pltpu.make_async_copy(buf.at[part, first + q, k], out_hbm.at[part, first + q, k], sem).start()

    gi_out.wait()
    pltpu.make_async_copy(buf, out_hbm, sem).wait()


def on_device(np_, nm, grid_input, preact, out_grad, mode_weight, local_weight):
    nb, na, nt, c = grid_input.shape
    _, nq, nk, _, _ = mode_weight.shape
    factor = 1.0 / (np_ * na * nt)
    consts = tables(np_, nm, nb, na, nt, nk, nq)
    unit = nm * nb * 2
    flat = lambda v: v.reshape(nb, na * nt, c)
    operands = (
        flat(preact), flat(out_grad), consts[0], flat(grid_input), *consts[1:], local_weight, mode_weight
    )
    anywhere = pl.BlockSpec(memory_space=pl.ANY)
    pos_buf = pltpu.VMEM((np_, nk, nb, 2 * na, c), BF16)
    mode_buf = pltpu.VMEM((nm, nk, nb * 2 * nq, c), BF16)
    owned = jax.ShapeDtypeStruct((nk, nq * unit, c), BF16)
    outs = (jax.ShapeDtypeStruct((nb, na * nt, c), BF16), owned, owned, owned)
    dma = pltpu.SemaphoreType.DMA
    sems = [dma((n, nk)) for n in (np_, np_, np_, np_, nm, nm, nm, nm, nm, nm, np_, np_)]
    grad_input, x_own, g1, g2 = pl.pallas_call(
        functools.partial(chain_kernel, np_, nm, factor),
        out_shape=outs,
        in_specs=[anywhere] * len(operands),
        out_specs=(anywhere,) * 4,
        scratch_shapes=[pltpu.VMEM(v.shape, BF16) for v in operands + outs]
        + [
            pltpu.VMEM((nb, na * nt, c), BF16),
            pltpu.VMEM((nb, na * nt, c), F32),
            pos_buf, pos_buf, pos_buf, pos_buf,
            mode_buf, mode_buf, mode_buf, mode_buf,
            pltpu.VMEM(owned.shape, BF16),
            mode_buf, mode_buf,
            pos_buf, pos_buf,
            dma((len(operands),)), dma((len(outs),)),
        ] + sems,
        compiler_params=pltpu.CompilerParams(
            collective_id=0, has_side_effects=True, vmem_limit_bytes=60 * 1024 * 1024
        ),
        name="chain",
    )(*operands)

    per_q = lambda v: v.reshape(nk, nq, unit, c)
    group = max(n for n in range(1, nq + 1) if nq % n == 0 and n * unit <= max(GROUP, unit))
    per_mode = pltpu.VMEM((nk, nq, unit, c), BF16)
    grad_modes, grad_input = pl.pallas_call(
        functools.partial(modes_kernel, group),
        out_shape=(jax.ShapeDtypeStruct(mode_weight.shape, BF16), outs[0]),
        in_specs=[anywhere] * 4,
        out_specs=(anywhere,) * 2,
        scratch_shapes=[
            per_mode, per_mode, per_mode,
            pltpu.VMEM(outs[0].shape, BF16),
            pltpu.VMEM(mode_weight.shape, BF16),
            dma((3, nk)), dma((2,)), dma(()),
        ],
        compiler_params=pltpu.CompilerParams(vmem_limit_bytes=60 * 1024 * 1024),
        name="modes",
    )(per_q(x_own), per_q(g1), per_q(g2), grad_input)
    return (grad_input.reshape(grid_input.shape), grad_modes)


def solution(mesh):
    return jax.shard_map(
        functools.partial(on_device, mesh.shape["pos"], mesh.shape["mode"]),
        mesh=mesh,
        in_specs=(
            P("mode", "pos", None, None),
            P("mode", "pos", None, None),
            P("mode", "pos", None, None),
            P(None, "mode", "pos", None, None),
            P(),
        ),
        out_specs=(P("mode", "pos", None, None), P(None, "mode", "pos", None, None)),
        check_vma=False,
    )
```

profile of v0, /device:TPU:0, one launch (start us, length us, event | category | flops | bytes accessed | tf_op | source)
XLA Modules:
  0.0 85.8 jit_solution(5628958058821414140)
XLA Ops:
  0.6 77.3 %chain.1 = (bf16[2,512,256]{2,1,0:T(8,128)(2,1)}, bf16[4,256,256]{2,1,0:T(8,128)(2,1)}, bf16[4,256,256]{2,1,0:T(8,128)(2,1)}, bf16[4,256,256]{2,1,0:T(8,128)(2,1)}) custom-call(bf16[2,512,256]{2,1,0:T(8,128)(2,1)} %bitcast.10, bf16[2,512,256]{2,1,0:T(8,128)(2,1)} %bitcast.11, bf16[4,256,512]{2,1,0:T(8,128)(2,1)} %constant.14.clone.tf_hbm, ...), custom_call_target="tpu_custom_call" | custom-call | tf_op jit(solution)/shard_map/chain/pallas_call | solution.py:291
  77.9 7.8 %modes.1 = (bf16[2,16,4,256,256]{4,3,2,1,0:T(8,128)(2,1)}, bf16[2,512,256]{2,1,0:T(8,128)(2,1)}) custom-call(bf16[4,16,16,256]{3,2,1,0:T(8,128)(2,1)} %bitcast.7, bf16[4,16,16,256]{3,2,1,0:T(8,128)(2,1)} %bitcast.8, bf16[4,16,16,256]{3,2,1,0:T(8,128)(2,1)} %bitcast.9, bf16[2,512,256]{2,1,0:T(8,128)(2,1)} %get-tuple-element.11.gi_hbm), custom_call_target="tpu_custom_call" | custom-call | tf_op jit(solution)/shard_map/modes/pallas_call | solution.py:316
where the time goes:
time: 85.9 us; the launch traced here: 85.8 us
  Pallas kernels  85.1 us (99%)
    pallas_call x1, Pallas kernels, on_device(): pl.pallas_call(functools.partial(chain_kernel, np_, nm, factor), out_shap...  77.3 us
    pallas_call x1, Pallas kernels, on_device(): pl.pallas_call(functools.partial(modes_kernel, group), out_shape=(jax.Sha...  7.85 us

commit v1 on v0

v1 whole, which is shorter than its diff:
```python
import functools
import math

import jax
import jax.numpy as jnp
import ml_dtypes
import numpy as np
from jax import lax
from jax.experimental import pallas as pl
from jax.experimental.pallas import tpu as pltpu
from jax.sharding import PartitionSpec as P

MESH = pl.DeviceIdType.MESH
F32 = jnp.float32
BF16 = jnp.bfloat16
GROUP = 128


def twiddle(length, mode_count):
    angles = (np.arange(length)[:, None] * np.arange(mode_count)[None, :] % length) * (2.0 * math.pi / length)
    as_bf16 = lambda v: v.astype(np.float32).astype(ml_dtypes.bfloat16).astype(np.float32)
    return as_bf16(np.cos(angles)), as_bf16(np.sin(angles))


def tables(np_, nm, nb, na, nt, nk, nq):
    cos_t, sin_t = twiddle(nt, np_ * nk)
    cos_s, sin_s = twiddle(np_ * na, nm * nq)
    eye_a, eye_b, eye_m, eye_q = np.eye(na), np.eye(nb), np.eye(nm), np.eye(nq)
    out = lambda v, *shape: jnp.asarray(v.reshape(shape).astype(ml_dtypes.bfloat16))
    by_k = np.stack([cos_t, -sin_t])
    by_k = by_k.reshape(2, nt, np_, nk)
    time_fwd = np.einsum("rtpk,ab->kprabt", by_k, eye_a)
    time_far = np.einsum("rtpk,ab->patkrb", by_k, eye_a)
    fwd = np.stack([np.stack([cos_s, sin_s]), np.stack([-sin_s, cos_s])])
    fwd = fwd.reshape(2, 2, np_, na, nm, nq)
    space_fwd = np.einsum("rspamq,bc->mbrqpcsa", fwd, eye_b)
    pick = np.einsum("rs,qu,mn,bc->qrmbncsu", np.eye(2), eye_q, eye_m, eye_b)
    turn = np.einsum("rs,qu,mn,bc->qrmbncsu", np.array([[0.0, 1.0], [-1.0, 0.0]]), eye_q, eye_m, eye_b)
    rows = nm * nb * 2 * nq
    return (
        out(time_fwd, nk, np_ * 2 * na, na * nt),
        out(space_fwd, rows, np_ * nb * 2 * na),
        out(pick, rows, rows),
        out(turn, rows, rows),
        out(time_far, np_, na * nt, nk * 2 * na),
    )


def dot(a, b):
    return jnp.dot(a, b, preferred_element_type=F32)


def dot_t(a, b):
    return lax.dot_general(a, b, (((1,), (1,)), ((), ())), preferred_element_type=F32)


def chain_kernel(
    np_, nm, factor,
    pre_hbm, og_hbm, tf_hbm, x_hbm, sf_hbm, pick_hbm, turn_hbm, lw_hbm, w_hbm,
    acc, far_hbm, xo_ref, g1_ref, g2_ref,
    pre_ref, og_ref, tf_ref, x_ref, sf_ref, pick_ref, turn_ref, lw_ref, w_buf, unpick_ref, si_ref, ti_ref,
    slope, gs, gr, xs, xr, ms, mr, ns, nr, bk, bs, br, ts, tr,
    in_sem, tf_sem, far_sem, g_ss, g_rs, x_ss, x_rs, m_ss, m_rs, n_ss, n_rs, b_ss, b_rs, t_ss, t_rs,
):
    nb, rows, c = slope.shape
    _, nk, _, ra, _ = gs.shape
    nq = w_buf.shape[1]
    unit = bk.shape[1] // nq
    pos, mode = lax.axis_index("pos"), lax.axis_index("mode")
    at = {"pos": pos, "mode": mode}
    size = {"pos": np_, "mode": nm}
    peer_of = lambda axis, d: lax.rem(at[axis] + d, size[axis])

    barrier = pltpu.get_barrier_semaphore()
    for axis in ("pos", "mode"):
        for d in range(1, size[axis]):
            pl.semaphore_signal(barrier, inc=1, device_id={axis: peer_of(axis, d)}, device_id_type=MESH)

    far = lax.rem(pos + np_ // 2, np_)
    hbm = (x_hbm, pre_hbm, og_hbm, sf_hbm, pick_hbm, turn_hbm, lw_hbm, w_hbm)
    local = (x_ref, pre_ref, og_ref, sf_ref, pick_ref, turn_ref, lw_ref, w_buf)
    loads = [pltpu.make_async_copy(h, v, in_sem.at[n]) for n, (h, v) in enumerate(zip(hbm, local))]
    tf_loads = [pltpu.make_async_copy(tf_hbm.at[k], tf_ref.at[k], tf_sem.at[k]) for k in range(nk)]
    for load in (loads[0], tf_loads[0], *loads[1:3], *tf_loads[1:], *loads[3:]):
        load.start()
    load_of = {id(v): load for v, load in zip(local, loads)}
    ready = lambda *refs: [load_of[id(r)].wait() for r in refs]

    step = 64

    def slope_step(i):
        b, r = i // (rows // step), pl.multiple_of(i % (rows // step) * step, step)
        values = pre_ref[b, pl.ds(r, step), :].astype(F32)
        cdf = 0.5 * (1.0 + lax.erf(values * 0.7071067811865476))
        density = jnp.exp(-0.5 * values * values) * 0.3989422804014327
        grad = og_ref[b, pl.ds(r, step), :].astype(F32)
        slope[b, pl.ds(r, step), :] = (grad * (cdf + values * density)).astype(BF16)

    def copy(axis, peer, slot, k, src, dst, ss, rs):
        return pltpu.make_async_remote_copy(
            src_ref=src.at[peer, k], dst_ref=dst.at[slot, k], send_sem=ss.at[peer, k], recv_sem=rs.at[slot, k],
            device_id={axis: peer}, device_id_type=MESH,
        )

    def peers(axis, skip, act):
        half = size[axis] // 2
        for first, last in ((1, half), (half + 1, size[axis])) if skip else ((1, size[axis]),):
            if first < last:
                pl.loop(first, last)(lambda d: act(peer_of(axis, d)))

    def send(axis, k, src, dst, ss, rs, skip=False):
        peers(axis, skip, lambda peer: copy(axis, peer, at[axis], k, src, dst, ss, rs).start())
        dst[at[axis], k] = src[at[axis], k]

    def arrive(axis, k, src, dst, ss, rs, skip=False):
        peers(axis, skip, lambda peer: copy(axis, peer, peer, k, src, dst, ss, rs).wait_recv())

    def drain(axis, k, src, dst, ss, rs, skip=False):
        peers(axis, skip, lambda peer: copy(axis, peer, peer, k, src, dst, ss, rs).wait_send())

    g_way = ("pos", gs, gr, g_ss, g_rs)
    x_way = ("pos", xs, xr, x_ss, x_rs)
    m_way = ("mode", ms, mr, m_ss, m_rs)
    n_way = ("mode", ns, nr, n_ss, n_rs)
    b_way = ("mode", bs, br, b_ss, b_rs)
    t_way = ("pos", ts, tr, t_ss, t_rs, True)
    go = lambda act, k, way: act(way[0], k, *way[1:])

    def time_fwd(source, buf, k):
        for b in range(nb):
            buf[:, k, b] = dot(tf_ref[k], source[b]).astype(BF16).reshape(np_, ra, c)

    def space_fwd(source, buf, k, scale):
        res = dot(sf_ref[...], source[:, k].reshape(-1, c))
        if scale != 1.0:
            res = res * scale
        buf[:, k] = res.astype(BF16).reshape(nm, -1, c)

    def gathered(buf, k):
        return buf[:, k].reshape(-1, c)

    ready(x_ref)
    tf_loads[0].wait()
    time_fwd(x_ref, xs, 0)
    pl.semaphore_wait(barrier, np_ - 1 + nm - 1)
    go(send, 0, x_way)
    ready(pre_ref, og_ref)
    pl.loop(0, nb * (rows // step))(slope_step)
    for k in range(nk):
        if k:
            tf_loads[k].wait()
        time_fwd(slope, gs, k)
        go(send, k, g_way)
    for k in range(1, nk):
        time_fwd(x_ref, xs, k)
    tr[far] = jnp.zeros(tr.shape[1:], BF16)
    ready(sf_ref, pick_ref, turn_ref, lw_ref, w_buf)
    unpick_ref[...] = pick_ref[...].T
    si_ref[...] = sf_ref[...].T
    for k in range(nk):
        ti_ref[k] = tf_ref[k].T

    far_copy = lambda k: pltpu.make_async_copy(ts.at[far, k], far_hbm.at[:, k], far_sem.at[k])

    def stage_space(k):
        go(arrive, k, g_way)
        go(drain, k, g_way)
        if k + 1 < nk:
            go(send, k + 1, x_way)
        space_fwd(gr, ms, k, factor)
        go(send, k, m_way)

    def stage_back(k):
        go(arrive, k, m_way)
        field = gathered(mr, k)
        g1_ref[k] = dot(pick_ref[...], field).astype(BF16)
        g2_ref[k] = dot(turn_ref[...], field).astype(BF16)

        @pl.loop(0, nq, unroll=math.gcd(nq, 4))
        def _(q):
            span = pl.ds(pl.multiple_of(q * unit, unit), unit)
            back = dot_t(g1_ref[k, span, :], w_buf[0, q, k]) + dot_t(g2_ref[k, span, :], w_buf[1, q, k])
            bk[k, span, :] = back.astype(BF16)

        bs[:, k] = dot(unpick_ref[...], bk[k]).astype(BF16).reshape(nm, -1, c)
        go(send, k, b_way)

    def stage_spread(k):
        go(arrive, k, b_way)
        spread = dot(si_ref[...], gathered(br, k)).astype(BF16)
        ts[:, k] = spread.reshape(np_, nb, ra, c)
        go(send, k, t_way)
        far_copy(k).start()

    def stage_x(k):
        go(arrive, k, x_way)
        space_fwd(xr, ns, k, 1.0)
        go(send, k, n_way)

    def stage_own(k):
        go(arrive, k, n_way)
        xo_ref[k] = dot(pick_ref[...], gathered(nr, k)).astype(BF16)

    def staged(*stages):
        for n in range(nk + len(stages) - 1):
            for lag, stage in enumerate(stages):
                if 0 <= n - lag < nk:
                    stage(n - lag)

    staged(stage_space, stage_back, stage_spread)
    for b in range(nb):
        acc[b] = dot_t(slope[b], lw_ref[...])
    staged(stage_x, stage_own)
    for k in range(nk):
        for way in (x_way, m_way, n_way, b_way):
            go(drain, k, way)

    for k in range(nk):
        go(arrive, k, t_way)
        for b in range(nb):
            acc[b] = acc[b] + dot(ti_ref[k], tr[:, k, b].reshape(-1, c))
    for k in range(nk):
        go(drain, k, t_way)
        far_copy(k).wait()


def modes_kernel(group, x_ref, g1_ref, g2_ref, out_hbm, buf, sem):
    nk, nq, unit, c = x_ref.shape

    @pl.loop(0, nk)
    def _(k):
        @pl.loop(0, nq // group)
        def _(i):
            first = i * group
            turned = x_ref[k, pl.ds(first, group)].reshape(group * unit, c).T
            for q in range(group):
                for part, g_ref in enumerate((g1_ref, g2_ref)):
                    rows = [jnp.zeros((n * unit, c), BF16) if n else None for n in (q, group - 1 - q)]
                    rows = [v for v in (rows[0], g_ref[k, first + q], rows[1]) if v is not None]
                    field = jnp.concatenate(rows, axis=0) if len(rows) > 1 else rows[0]
                    buf[part, first + q, k] = dot(turned, field).astype(BF16)
                    pltpu.make_async_copy(buf.at[part, first + q, k], out_hbm.at[part, first + q, k], sem).start()

    pltpu.make_async_copy(buf, out_hbm, sem).wait()


def finish_kernel(np_, acc_ref, far_ref, tab_hbm, out_hbm, tab_ref, out_ref, in_sem, out_sem):
    nb = acc_ref.shape[0]
    peer = lax.rem(lax.axis_index("pos") + np_ // 2, np_)
    tab = pltpu.make_async_copy(tab_hbm.at[peer], tab_ref, in_sem)
    outs = [pltpu.make_async_copy(out_ref.at[b], out_hbm.at[b], out_sem.at[b]) for b in range(nb)]
    tab.start()
    tab.wait()
    for b in range(nb):
        out_ref[b] = (acc_ref[b] + dot(tab_ref[...], far_ref[b])).astype(BF16)
        outs[b].start()
    for b in range(nb):
        outs[b].wait()


def on_device(np_, nm, grid_input, preact, out_grad, mode_weight, local_weight):
    nb, na, nt, c = grid_input.shape
    _, nq, nk, _, _ = mode_weight.shape
    factor = 1.0 / (np_ * na * nt)
    consts = tables(np_, nm, nb, na, nt, nk, nq)
    unit = nm * nb * 2
    flat = lambda v: v.reshape(nb, na * nt, c)
    operands = (
        flat(preact), flat(out_grad), consts[0], flat(grid_input), *consts[1:-1], local_weight, mode_weight
    )
    anywhere = pl.BlockSpec(memory_space=pl.ANY)
    on_chip = pl.BlockSpec(memory_space=pltpu.VMEM)
    in_place = pl.BlockSpec(memory_space=pltpu.HBM)
    pos_buf = pltpu.VMEM((np_, nk, nb, 2 * na, c), BF16)
    mode_buf = pltpu.VMEM((nm, nk, nb * 2 * nq, c), BF16)
    owned = jax.ShapeDtypeStruct((nk, nq * unit, c), BF16)
    field = jax.ShapeDtypeStruct((nb, na * nt, c), BF16)
    total = jax.ShapeDtypeStruct(field.shape, F32)
    far = jax.ShapeDtypeStruct((nb, nk, 2 * na, c), BF16)
    dma = pltpu.SemaphoreType.DMA
    sems = [dma((n, nk)) for n in (np_, np_, np_, np_, nm, nm, nm, nm, nm, nm, np_, np_)]
    acc, far, x_own, g1, g2 = pl.pallas_call(
        functools.partial(chain_kernel, np_, nm, factor),
        out_shape=(total, far, owned, owned, owned),
        in_specs=[in_place] * len(operands),
        out_specs=(on_chip, anywhere, on_chip, on_chip, on_chip),
        scratch_shapes=[pltpu.VMEM(v.shape, BF16) for v in operands]
        + [
            pltpu.VMEM(consts[2].shape, BF16),
            pltpu.VMEM(consts[1].shape[::-1], BF16),
            pltpu.VMEM((nk, na * nt, np_ * 2 * na), BF16),
            pltpu.VMEM(field.shape, BF16),
            pos_buf, pos_buf, pos_buf, pos_buf,
            mode_buf, mode_buf, mode_buf, mode_buf,
            pltpu.VMEM(owned.shape, BF16),
            mode_buf, mode_buf,
            pos_buf, pos_buf,
            dma((len(operands),)), dma((nk,)), dma((nk,)),
        ] + sems,
        compiler_params=pltpu.CompilerParams(
            collective_id=0, has_side_effects=True, vmem_limit_bytes=40 * 1024 * 1024
        ),
        name="chain",
    )(*[pltpu.with_memory_space_constraint(v, pltpu.HBM) for v in operands])

    far = lax.ppermute(far, "pos", [(n, (n + np_ // 2) % np_) for n in range(np_)])
    per_q = lambda v: v.reshape(nk, nq, unit, c)
    group = max(n for n in range(1, nq + 1) if nq % n == 0 and n * unit <= max(GROUP, unit))
    grad_modes = pl.pallas_call(
        functools.partial(modes_kernel, group),
        out_shape=jax.ShapeDtypeStruct(mode_weight.shape, BF16),
        in_specs=[on_chip] * 3,
        out_specs=anywhere,
        scratch_shapes=[pltpu.VMEM(mode_weight.shape, BF16), dma(())],
        cost_estimate=pl.CostEstimate(
            flops=2 * unit * mode_weight.size, bytes_accessed=2 * mode_weight.size, transcendentals=0
        ),
        compiler_params=pltpu.CompilerParams(vmem_limit_bytes=24 * 1024 * 1024),
        name="modes",
    )(per_q(x_own), per_q(g1), per_q(g2))
    grad_input = pl.pallas_call(
        functools.partial(finish_kernel, np_),
        out_shape=field,
        in_specs=[on_chip, on_chip, in_place],
        out_specs=anywhere,
        scratch_shapes=[
            pltpu.VMEM(consts[-1].shape[1:], BF16),
            pltpu.VMEM(field.shape, BF16),
            dma(()), dma((nb,)),
        ],
        compiler_params=pltpu.CompilerParams(vmem_limit_bytes=16 * 1024 * 1024),
        name="finish",
    )(acc, far.reshape(nb, nk * 2 * na, c), consts[-1])
    return (grad_input.reshape(grid_input.shape), grad_modes)


def solution(mesh):
    return jax.shard_map(
        functools.partial(on_device, mesh.shape["pos"], mesh.shape["mode"]),
        mesh=mesh,
        in_specs=(
            P("mode", "pos", None, None),
            P("mode", "pos", None, None),
            P("mode", "pos", None, None),
            P(None, "mode", "pos", None, None),
            P(),
        ),
        out_specs=(P("mode", "pos", None, None), P(None, "mode", "pos", None, None)),
        check_vma=False,
    )
```

time: 85.9 us -> 81.3 us (0.946)
  Pallas kernels: 85.1 us -> 77.6 us
  starting transfers between devices: 0 us -> 2.85 us
    pallas_call x1, Pallas kernels: 77.3 us -> 69.7 us  [on_device(): pl.pallas_call(functools.partial(chain_kernel, np_, nm, factor), out_shap...]
    ppermute x0 -> x1, starting transfers between devices: none -> 2.85 us  [on_device(): lax.ppermute(far, 'pos', [(n, (n + np_ // 2) % np_) for n in range(np_)])]
    pallas_call x1 -> x2, Pallas kernels: 7.85 us -> 7.96 us  [the longest x1 6.68 us: on_device(): pl.pallas_call(functools.partial(modes_kernel, group), out_shape=jax.Shap...]
  transfers between devices with their start and end apart: 0 -> 1, of which waited for: 0 -> 0; matrix products, arithmetic and copies ran while one was open for 0% -> 0% of each run, Pallas kernels for 0% -> 8%
where the time goes in v1:
time: 81.3 us; the launch traced here: 81.2 us
  Pallas kernels  77.6 us (95%)
  starting transfers between devices  2.85 us (4%)
    pallas_call x1, Pallas kernels, on_device(): pl.pallas_call(functools.partial(chain_kernel, np_, nm, factor), out_shap...  69.7 us
    pallas_call x1, Pallas kernels, on_device(): pl.pallas_call(functools.partial(modes_kernel, group), out_shape=jax.Shap...  6.68 us
    ppermute x1, starting transfers between devices, on_device(): lax.ppermute(far, 'pos', [(n, (n + np_ // 2) % np_) for n in range(np_)])  2.85 us
  transfers between devices with their start and end apart: 1, of which 0 were waited for; matrix products, arithmetic and copies ran while one was open for 0% of the time, Pallas kernels for 8%

profile of v1, /device:TPU:0, one launch (start us, length us, event | category | flops | bytes accessed | tf_op | source)
XLA Modules:
  0.0 81.2 jit_solution(5341365785897441597)
XLA Ops:
  0.6 0.0 copy-start
  0.6 69.7 %chain.1 = (f32[2,512,256]{2,1,0:T(8,128)S(1)}, bf16[2,4,32,256]{3,2,1,0:T(8,128)(2,1)S(1)}, bf16[4,256,256]{2,1,0:T(8,128)(2,1)S(1)}, bf16[4,256,256]{2,1,0:T(8,128)(2,1)S(1)}, bf16[4,256,256]{2,1,0:T(8,128)(2,1)S(1)}) custom-call(bf16[2,512,256]{2,1,0:T(8,128)(2,1)} %bitcast.12, bf16[2,512,256]{2,1,0:T(8,128)(2,1)} %bitcast.13, ...), custom_call_target="tpu_custom_call" | custom-call | tf_op jit(solution)/shard_map/chain/pallas_call | solution.py:282
  70.3 2.8 %collective-permute-start = (bf16[2,4,32,256]{3,2,1,0:T(8,128)(2,1)S(1)}, bf16[2,4,32,256]{3,2,1,0:T(8,128)(2,1)S(1)}, u32[]{:S(2)}, u32[]{:S(2)}) collective-permute-start(bf16[2,4,32,256]{3,2,1,0:T(8,128)(2,1)S(1)} %get-tuple-element.8), channel_id=1, source_target_pairs={{0,16},{4,20},{8,24},{12,28},{16,0},{20,4},{24,8},{28,12},{1,17},{... | collective-permute-start | bytes 393224 | tf_op jit(solution)/shard_map/ppermute | solution.py:306
  73.2 6.7 %modes.1 = bf16[2,16,4,256,256]{4,3,2,1,0:T(8,128)(2,1)} custom-call(bf16[4,16,16,256]{3,2,1,0:T(8,128)(2,1)S(1)} %bitcast.8, bf16[4,16,16,256]{3,2,1,0:T(8,128)(2,1)S(1)} %bitcast.9, bf16[4,16,16,256]{3,2,1,0:T(8,128)(2,1)S(1)} %bitcast.10), custom_call_target="tpu_custom_call" | custom-call | flops 268435456 | bytes 16777216 | tf_op jit(solution)/shard_map/modes/pallas_call | solution.py:309
  79.9 0.0 collective-permute-done
  79.9 0.0 copy-done
  79.9 1.3 %finish.1 = bf16[2,512,256]{2,1,0:T(8,128)(2,1)} custom-call(f32[2,512,256]{2,1,0:T(8,128)S(1)} %get-tuple-element.7.acc_ref, bf16[2,128,256]{2,1,0:T(8,128)(2,1)S(1)} %bitcast.11, bf16[8,512,128]{2,1,0:T(8,128)(2,1)S(1)} %copy-done), custom_call_target="tpu_custom_call" | custom-call | tf_op jit(solution)/shard_map/finish/pallas_call | solution.py:321
Async XLA Ops:
  0.6 79.3 %copy-start = (bf16[8,512,128]{2,1,0:T(8,128)(2,1)S(1)}, bf16[8,512,128]{2,1,0:T(8,128)(2,1)}, u32[]{:S(2)}) copy-start(bf16[8,512,128]{2,1,0:T(8,128)(2,1)} %constant.14.clone.tab_hbm) | copy-start | bytes 3145732
  70.3 9.5 %collective-permute-start = (bf16[2,4,32,256]{3,2,1,0:T(8,128)(2,1)S(1)}, bf16[2,4,32,256]{3,2,1,0:T(8,128)(2,1)S(1)}, u32[]{:S(2)}, u32[]{:S(2)}) collective-permute-start(bf16[2,4,32,256]{3,2,1,0:T(8,128)(2,1)S(1)} %get-tuple-element.8), channel_id=1, source_target_pairs={{0,16},{4,20},{8,24},{12,28},{16,0},{20,4},{24,8},{28,12},{1,17},{... | collective-permute-start | bytes 393224 | tf_op jit(solution)/shard_map/ppermute | solution.py:306

commit v2 on v1

--- a/solution.py
+++ b/solution.py
@@ -153,6 +153,7 @@
         go(send, k, g_way)
     for k in range(1, nk):
         time_fwd(x_ref, xs, k)
+        go(send, k, x_way)
     tr[far] = jnp.zeros(tr.shape[1:], BF16)
     ready(sf_ref, pick_ref, turn_ref, lw_ref, w_buf)
     unpick_ref[...] = pick_ref[...].T
@@ -165,8 +166,6 @@
     def stage_space(k):
         go(arrive, k, g_way)
         go(drain, k, g_way)
-        if k + 1 < nk:
-            go(send, k + 1, x_way)
         space_fwd(gr, ms, k, factor)
         go(send, k, m_way)
 

time: 81.3 us -> 81.2 us (level)
  no operation moved by 1% of the time
where the time goes in v2:
time: 81.2 us; the launch traced here: 81.1 us
  Pallas kernels  77.5 us (95%)
  starting transfers between devices  2.91 us (4%)
    pallas_call x1, Pallas kernels, on_device(): pl.pallas_call(functools.partial(chain_kernel, np_, nm, factor), out_shap...  69.6 us
    pallas_call x1, Pallas kernels, on_device(): pl.pallas_call(functools.partial(modes_kernel, group), out_shape=jax.Shap...  6.67 us
    ppermute x1, starting transfers between devices, on_device(): lax.ppermute(far, 'pos', [(n, (n + np_ // 2) % np_) for n in range(np_)])  2.91 us
  transfers between devices with their start and end apart: 1, of which 0 were waited for; matrix products, arithmetic and copies ran while one was open for 0% of the time, Pallas kernels for 8%

profile of v2, /device:TPU:0, one launch (start us, length us, event | category | flops | bytes accessed | tf_op | source)
XLA Modules:
  0.0 81.1 jit_solution(17342943327829024910)
XLA Ops:
  0.6 0.0 copy-start
  0.6 69.6 %chain.1 = (f32[2,512,256]{2,1,0:T(8,128)S(1)}, bf16[2,4,32,256]{3,2,1,0:T(8,128)(2,1)S(1)}, bf16[4,256,256]{2,1,0:T(8,128)(2,1)S(1)}, bf16[4,256,256]{2,1,0:T(8,128)(2,1)S(1)}, bf16[4,256,256]{2,1,0:T(8,128)(2,1)S(1)}) custom-call(bf16[2,512,256]{2,1,0:T(8,128)(2,1)} %bitcast.12, bf16[2,512,256]{2,1,0:T(8,128)(2,1)} %bitcast.13, ...), custom_call_target="tpu_custom_call" | custom-call | tf_op jit(solution)/shard_map/chain/pallas_call | solution.py:281
  70.2 2.9 %collective-permute-start = (bf16[2,4,32,256]{3,2,1,0:T(8,128)(2,1)S(1)}, bf16[2,4,32,256]{3,2,1,0:T(8,128)(2,1)S(1)}, u32[]{:S(2)}, u32[]{:S(2)}) collective-permute-start(bf16[2,4,32,256]{3,2,1,0:T(8,128)(2,1)S(1)} %get-tuple-element.8), channel_id=1, source_target_pairs={{0,16},{4,20},{8,24},{12,28},{16,0},{20,4},{24,8},{28,12},{1,17},{... | collective-permute-start | bytes 393224 | tf_op jit(solution)/shard_map/ppermute | solution.py:305
  73.1 6.7 %modes.1 = bf16[2,16,4,256,256]{4,3,2,1,0:T(8,128)(2,1)} custom-call(bf16[4,16,16,256]{3,2,1,0:T(8,128)(2,1)S(1)} %bitcast.8, bf16[4,16,16,256]{3,2,1,0:T(8,128)(2,1)S(1)} %bitcast.9, bf16[4,16,16,256]{3,2,1,0:T(8,128)(2,1)S(1)} %bitcast.10), custom_call_target="tpu_custom_call" | custom-call | flops 268435456 | bytes 16777216 | tf_op jit(solution)/shard_map/modes/pallas_call | solution.py:308
  79.8 0.0 collective-permute-done
  79.8 0.0 copy-done
  79.8 1.3 %finish.1 = bf16[2,512,256]{2,1,0:T(8,128)(2,1)} custom-call(f32[2,512,256]{2,1,0:T(8,128)S(1)} %get-tuple-element.7.acc_ref, bf16[2,128,256]{2,1,0:T(8,128)(2,1)S(1)} %bitcast.11, bf16[8,512,128]{2,1,0:T(8,128)(2,1)S(1)} %copy-done), custom_call_target="tpu_custom_call" | custom-call | tf_op jit(solution)/shard_map/finish/pallas_call | solution.py:320
Async XLA Ops:
  0.6 79.2 %copy-start = (bf16[8,512,128]{2,1,0:T(8,128)(2,1)S(1)}, bf16[8,512,128]{2,1,0:T(8,128)(2,1)}, u32[]{:S(2)}) copy-start(bf16[8,512,128]{2,1,0:T(8,128)(2,1)} %constant.14.clone.tab_hbm) | copy-start | bytes 3145732
  70.2 9.6 %collective-permute-start = (bf16[2,4,32,256]{3,2,1,0:T(8,128)(2,1)S(1)}, bf16[2,4,32,256]{3,2,1,0:T(8,128)(2,1)S(1)}, u32[]{:S(2)}, u32[]{:S(2)}) collective-permute-start(bf16[2,4,32,256]{3,2,1,0:T(8,128)(2,1)S(1)} %get-tuple-element.8), channel_id=1, source_target_pairs={{0,16},{4,20},{8,24},{12,28},{16,0},{20,4},{24,8},{28,12},{1,17},{... | collective-permute-start | bytes 393224 | tf_op jit(solution)/shard_map/ppermute | solution.py:305

commit v3 on v2

--- a/solution.py
+++ b/solution.py
@@ -109,7 +109,21 @@
                 pl.loop(first, last)(lambda d: act(peer_of(axis, d)))
 
     def send(axis, k, src, dst, ss, rs, skip=False):
-        peers(axis, skip, lambda peer: copy(axis, peer, at[axis], k, src, dst, ss, rs).start())
+        if skip and size[axis] % 4 == 0:
+            quarter = size[axis] // 4
+
+            @pl.loop(0, size[axis])
+            def _(i):
+                block = i // quarter
+                base = jnp.where(block < 2, block * 2, block * 2 - 3) * quarter
+                peer = base + lax.rem(i + at[axis], quarter)
+                there = jnp.logical_and(peer != at[axis], peer != lax.rem(at[axis] + size[axis] // 2, size[axis]))
+
+                @pl.when(there)
+                def _():
+                    copy(axis, peer, at[axis], k, src, dst, ss, rs).start()
+        else:
+            peers(axis, skip, lambda peer: copy(axis, peer, at[axis], k, src, dst, ss, rs).start())
         dst[at[axis], k] = src[at[axis], k]
 
     def arrive(axis, k, src, dst, ss, rs, skip=False):

time: 81.2 us -> 81.2 us (level)
  no operation moved by 1% of the time
where the time goes in v3:
time: 81.2 us; the launch traced here: 81.1 us
  Pallas kernels  77.6 us (96%)
  starting transfers between devices  2.81 us (3%)
    pallas_call x1, Pallas kernels, on_device(): pl.pallas_call(functools.partial(chain_kernel, np_, nm, factor), out_shap...  69.6 us
    pallas_call x1, Pallas kernels, on_device(): pl.pallas_call(functools.partial(modes_kernel, group), out_shape=jax.Shap...  6.68 us
    ppermute x1, starting transfers between devices, on_device(): lax.ppermute(far, 'pos', [(n, (n + np_ // 2) % np_) for n in range(np_)])  2.81 us
  transfers between devices with their start and end apart: 1, of which 0 were waited for; matrix products, arithmetic and copies ran while one was open for 0% of the time, Pallas kernels for 8%

profile of v3, /device:TPU:0, one launch (start us, length us, event | category | flops | bytes accessed | tf_op | source)
XLA Modules:
  0.0 81.1 jit_solution(18050761092688565496)
XLA Ops:
  0.6 0.0 copy-start
  0.6 69.6 %chain.1 = (f32[2,512,256]{2,1,0:T(8,128)S(1)}, bf16[2,4,32,256]{3,2,1,0:T(8,128)(2,1)S(1)}, bf16[4,256,256]{2,1,0:T(8,128)(2,1)S(1)}, bf16[4,256,256]{2,1,0:T(8,128)(2,1)S(1)}, bf16[4,256,256]{2,1,0:T(8,128)(2,1)S(1)}) custom-call(bf16[2,512,256]{2,1,0:T(8,128)(2,1)} %bitcast.12, bf16[2,512,256]{2,1,0:T(8,128)(2,1)} %bitcast.13, ...), custom_call_target="tpu_custom_call" | custom-call | tf_op jit(solution)/shard_map/chain/pallas_call | solution.py:295
  70.3 2.8 %collective-permute-start = (bf16[2,4,32,256]{3,2,1,0:T(8,128)(2,1)S(1)}, bf16[2,4,32,256]{3,2,1,0:T(8,128)(2,1)S(1)}, u32[]{:S(2)}, u32[]{:S(2)}) collective-permute-start(bf16[2,4,32,256]{3,2,1,0:T(8,128)(2,1)S(1)} %get-tuple-element.8), channel_id=1, source_target_pairs={{0,16},{4,20},{8,24},{12,28},{16,0},{20,4},{24,8},{28,12},{1,17},{... | collective-permute-start | bytes 393224 | tf_op jit(solution)/shard_map/ppermute | solution.py:319
  73.1 6.7 %modes.1 = bf16[2,16,4,256,256]{4,3,2,1,0:T(8,128)(2,1)} custom-call(bf16[4,16,16,256]{3,2,1,0:T(8,128)(2,1)S(1)} %bitcast.8, bf16[4,16,16,256]{3,2,1,0:T(8,128)(2,1)S(1)} %bitcast.9, bf16[4,16,16,256]{3,2,1,0:T(8,128)(2,1)S(1)} %bitcast.10), custom_call_target="tpu_custom_call" | custom-call | flops 268435456 | bytes 16777216 | tf_op jit(solution)/shard_map/modes/pallas_call | solution.py:322
  79.8 0.0 collective-permute-done
  79.8 0.0 copy-done
  79.8 1.3 %finish.1 = bf16[2,512,256]{2,1,0:T(8,128)(2,1)} custom-call(f32[2,512,256]{2,1,0:T(8,128)S(1)} %get-tuple-element.7.acc_ref, bf16[2,128,256]{2,1,0:T(8,128)(2,1)S(1)} %bitcast.11, bf16[8,512,128]{2,1,0:T(8,128)(2,1)S(1)} %copy-done), custom_call_target="tpu_custom_call" | custom-call | tf_op jit(solution)/shard_map/finish/pallas_call | solution.py:334
Async XLA Ops:
  0.6 79.1 %copy-start = (bf16[8,512,128]{2,1,0:T(8,128)(2,1)S(1)}, bf16[8,512,128]{2,1,0:T(8,128)(2,1)}, u32[]{:S(2)}) copy-start(bf16[8,512,128]{2,1,0:T(8,128)(2,1)} %constant.14.clone.tab_hbm) | copy-start | bytes 3145732
  70.3 9.5 %collective-permute-start = (bf16[2,4,32,256]{3,2,1,0:T(8,128)(2,1)S(1)}, bf16[2,4,32,256]{3,2,1,0:T(8,128)(2,1)S(1)}, u32[]{:S(2)}, u32[]{:S(2)}) collective-permute-start(bf16[2,4,32,256]{3,2,1,0:T(8,128)(2,1)S(1)} %get-tuple-element.8), channel_id=1, source_target_pairs={{0,16},{4,20},{8,24},{12,28},{16,0},{20,4},{24,8},{28,12},{1,17},{... | collective-permute-start | bytes 393224 | tf_op jit(solution)/shard_map/ppermute | solution.py:319
